TPU v7x, 128 devices: a whole 4x4x4 slice. The times are simulated.
128 devices in a mesh: sub: 16 (over z, y_hi, core), tile: 8 (over y_lo, x).
Axes of the slice: x: 4, y: 4 (y_hi: 2, y_lo: 2; y = y_hi * 2 + y_lo), z: 4, core: 2. Of those that a mesh axis runs over, the one named last changes fastest.
Arguments:
- load_current: float32 [16, 2, 512, 4096], P('sub', None, 'tile'), may hold values from -6 to 6
- diagonal: float32 [16, 2, 512, 4096], P('sub', None, 'tile')
- start_field: float32 [16, 2, 512, 4096], P('sub', None, 'tile'), may hold values from -4 to 4
- block_inverse: float32 [16, 16, 2, 256, 2, 256], P('sub')
- multipliers: float32 [16, 2, 512, 128], P('sub', None, 'tile'), may hold values from -6 to 6
- active_rows: int32 [16], replicated, may hold values from 128 to 512, as said below
- contact_peer: int32 [16, 8], replicated, may hold values from 0 to 15, as said below
- contact_len: int32 [16, 8], replicated, may hold values from 1 to 256, 512 in all within a row
- port_row: int32 [16, 16], P('sub'), may hold values from 0 to 511
- port_col: int32 [16, 16], P('sub'), may hold values from 0 to 3968
- port_current: float32 [16, 2, 16], P('sub'), may hold values from -16 to 16
Outputs:
- solution: float32 [16, 2, 512, 4096], P('sub', None, 'tile')
- next_multipliers: float32 [16, 2, 512, 128], P('sub', None, 'tile')
Inputs may be any that keep to these rules, and one draw needn't show every extreme that they name: `active_rows`: at least one subdomain has all 512 lines active. `contact_peer`: a contact never names its own subdomain.
All inputs are finite; a program needn't handle non-finite values.
Results may differ from a plain program's by a relative error of at most 0.0003.
Values sent between devices are 32-bit elements; how exact they have to be, the bound alone decides.
A program may use at most 128 MiB of HBM per device.

v0:
```python
import functools

import jax
import jax.numpy as jnp
from jax import lax
from jax.experimental import pallas as pl
from jax.experimental.pallas import tpu as pltpu
from jax.sharding import PartitionSpec as P

MESH = pl.DeviceIdType.MESH
BF = jnp.bfloat16
F32 = jnp.float32
NB = 16
ROWS = 64
EARLY = 5
AHEAD = 4

RUNS = (
    (0, 0, 1, 15),
    (1, 0, 1, 11),
    (0, 15, 1, 1),
    (1, 11, 1, 2),
    (2, 0, 1, 4),
    (1, 15, -1, 3),
    (2, 4, 1, 4),
    (2, 15, 1, 1),
    (2, 8, 1, 7),
)
ORDER = [(s, k0 + d * i) for s, k0, d, n in RUNS for i in range(n)]
TOTAL = len(ORDER)
AT = {entry: e for e, entry in enumerate(ORDER)}
AT_INFLOW = AT[(0, 15)]
AT_FAR = AT[(2, 15)]


def check_order():
    assert sorted(ORDER) == [(s, k) for s in range(3) for k in range(NB)]
    for s, k in ORDER:
        if s:
            for j in (k - 1, k, k + 1):
                if 0 <= j < NB:
                    assert AT[(s - 1, j)] + 2 <= AT[(s, k)]


def entry_of(e):
    sweep = jnp.int32(RUNS[0][0])
    block = RUNS[0][1] + RUNS[0][2] * e
    start = RUNS[0][3]
    for s, k0, d, n in RUNS[1:]:
        later = e >= start
        sweep = jnp.where(later, s, sweep)
        block = jnp.where(later, k0 + d * (e - start), block)
        start += n
    return sweep, block


def body(
    load_hbm, diag_hbm, start_hbm, edge_hbm, block_hbm, mult_hbm, active_ref,
    len_hbm, peer_hbm, prow_hbm, pcol_hbm, pcur_hbm,
    out_hbm, next_hbm,
    field, src, diag, stage, upper, lower, lhs,
    held, far, inflow, part, part_in, end_in, ahead_out,
    peers, lens, cpeer, prow, pcol, pcur, weights,
    in_sem, b_sem, small_sem, hs_sem, hr_sem, s1_sem, r1_sem, s2_sem, r2_sem, p_sem, o_sem, n_sem,
):
    sub = lax.axis_index("sub")
    tile = lax.axis_index("tile")
    last_tile = lax.axis_size("tile") - 1
    core = lax.rem(sub, 2)
    place = sub // 2
    places = lax.axis_size("sub") // 2
    partner = place * 2 + (1 - core)
    first_row = tile * ROWS
    has_up = tile > 0
    has_down = tile < last_tile

    def inputs_of(j):
        t = 2 * j
        copies = []
        for c in range(2):
            for h in range(2):
                copies.append(
                    pltpu.make_async_copy(
                        start_hbm.at[0, c, :, pl.ds(pl.multiple_of((t + h) * 128, 128), 128)],
                        field.at[0, c, t + h + 1, pl.ds(8, ROWS), :],
                        in_sem.at[j, 2 * c + h],
                    )
                )
        copies.append(
            pltpu.make_async_copy(
                load_hbm.at[:, :, pl.ds(t, 2)], src.at[:, :, pl.ds(t, 2)], in_sem.at[j, 4]
            )
        )
        copies.append(
            pltpu.make_async_copy(
                diag_hbm.at[:, :, pl.ds(t, 2)], diag.at[:, :, pl.ds(t, 2)], in_sem.at[j, 5]
            )
        )
        return copies

    def blocks_of(j):
        return pltpu.make_async_copy(block_hbm.at[j], stage.at[j], b_sem.at[j])

    def issue(j):
        for copy in inputs_of(j):
            copy.start()
        blocks_of(j).start()

    small = [
        pltpu.make_async_copy(a, b, small_sem.at[i])
        for i, (a, b) in enumerate(
            (
                (len_hbm, lens), (peer_hbm, cpeer), (prow_hbm, prow),
                (pcol_hbm, pcol), (pcur_hbm, pcur),
            )
        )
    ]
    own_mult = pltpu.make_async_copy(mult_hbm.at[0], held.at[place], small_sem.at[5])

    def edge_copy(side, s, k):
        t = 2 * k + 1
        row, there, to = ((8, ROWS + 8, tile - 1), (ROWS + 7, 7, tile + 1))[side]
        return pltpu.make_async_remote_copy(
            src_ref=field.at[s, :, pl.ds(t, 2), pl.ds(row, 1), :],
            dst_ref=field.at[s, :, pl.ds(t, 2), pl.ds(there, 1), :],
            send_sem=hs_sem.at[side, s, k],
            recv_sem=hr_sem.at[side, s, k],
            device_id=(sub, to),
            device_id_type=MESH,
        )

    def first_edge(side):
        group, line, there, to = ((0, 0, ROWS + 8, tile - 1), (7, 7, 7, tile + 1))[side]
        return pltpu.make_async_remote_copy(
            src_ref=edge_hbm.at[:, group, :, pl.ds(line, 1), :],
            dst_ref=field.at[0, :, pl.ds(1, 2 * NB), pl.ds(there, 1), :],
            send_sem=hs_sem.at[side, 0, 0],
            recv_sem=hr_sem.at[side, 0, 0],
            device_id=(sub, to),
            device_id_type=MESH,
        )

    def spread(source, target, send, recv, offset, slot):
        to = lax.rem(place + offset, places)
        return pltpu.make_async_remote_copy(
            src_ref=source,
            dst_ref=target.at[slot],
            send_sem=send.at[offset - 1],
            recv_sem=recv.at[slot],
            device_id=(to * 2 + core, tile),
            device_id_type=MESH,
        )

    def to_partner(source, target, which):
        return pltpu.make_async_remote_copy(
            src_ref=source,
            dst_ref=target,
            send_sem=p_sem.at[2 * which],
            recv_sem=p_sem.at[2 * which + 1],
            device_id=(partner, tile),
            device_id_type=MESH,
        )

    def far_source():
        return field.at[3, :, 2 * NB, pl.ds(8, ROWS), :]

    for copy in small:
        copy.start()
    for j in range(2):
        issue(j)
    own_mult.start()
    barrier = pltpu.get_barrier_semaphore()
    for offset in range(1, 8):
        to = lax.rem(place + offset, places)
        pl.semaphore_signal(barrier, inc=1, device_id=(to * 2 + core, tile), device_id_type=MESH)
    pl.semaphore_signal(barrier, inc=1, device_id=(partner, tile), device_id_type=MESH)

    @pl.when(has_up)
    def _():
        pl.semaphore_signal(barrier, inc=1, device_id=(sub, tile - 1), device_id_type=MESH)

    @pl.when(has_down)
    def _():
        pl.semaphore_signal(barrier, inc=1, device_id=(sub, tile + 1), device_id_type=MESH)

    for j in range(2, EARLY + AHEAD):
        issue(j)

    for s in range(3):
        for c in range(2):
            for t in (0, 2 * NB + 1):
                field[s, c, t, 8 : ROWS + 8, :] = jnp.zeros((ROWS, 128), F32)

    @pl.when(tile == 0)
    def _():
        for s in range(3):
            field[s, :, :, 7:8, :] = jnp.zeros((2, 2 * NB + 2, 1, 128), F32)

    @pl.when(tile == last_tile)
    def _():
        for s in range(3):
            field[s, :, :, ROWS + 8 : ROWS + 9, :] = jnp.zeros((2, 2 * NB + 2, 1, 128), F32)

    for copy in small:
        copy.wait()
    active = active_ref[sub]
    length = lens[...]
    ends = length
    depth = lax.broadcasted_iota(jnp.int32, length.shape, 0)
    for step in (1, 2, 4):
        ends = ends + jnp.where(depth >= step, pltpu.roll(ends, step, 0), 0)
    starts = ends - length
    named = cpeer[...]
    line16 = lax.broadcasted_iota(jnp.int32, (ROWS, 16), 0) + first_row
    found = jnp.zeros((ROWS, 16), jnp.int32)
    for c in range(8):
        inside = (line16 >= starts[c : c + 1, :]) & (line16 < ends[c : c + 1, :])
        found = found + jnp.where(inside, named[c : c + 1, :], 0)
    peers[...] = found.astype(F32)
    rows_hot = (prow[...] == line16).astype(F32)
    for c in range(2):
        weighted = rows_hot * pcur[c : c + 1, :]
        top = weighted.astype(BF)
        weights[c * ROWS : (c + 1) * ROWS, :] = top
        weights[(2 + c) * ROWS : (3 + c) * ROWS, :] = (weighted - top.astype(F32)).astype(BF)
    eye = lax.broadcasted_iota(jnp.int32, (16, 16), 0) == lax.broadcasted_iota(jnp.int32, (16, 16), 1)
    col = jnp.sum(jnp.where(eye, pcol[...].astype(F32), 0.0), axis=1, keepdims=True)

    def line_mask():
        line = lax.broadcasted_iota(jnp.int32, (ROWS, 128), 0) + first_row
        return (line < active).astype(F32)

    def split(j):
        for q in range(4):
            v = stage[j, pl.ds(q, 512, stride=4), :].T
            top = v.astype(BF)
            upper[j, q * 128 : (q + 1) * 128, :] = top
            lower[j, q * 128 : (q + 1) * 128, :] = (v - top.astype(F32)).astype(BF)

    def await_inputs(j):
        for copy in inputs_of(j):
            copy.wait()
        blocks_of(j).wait()

    def prepare(j):
        mask = line_mask()
        at = lax.broadcasted_iota(jnp.int32, (16, 256), 1).astype(F32) + (j * 256).astype(F32)
        cols_hot = ((at >= col) & (at < col + 128.0)).astype(F32).astype(BF)
        fed = jnp.dot(weights[...], cols_hot, preferred_element_type=F32)
        for c in range(2):
            for h in range(2):
                t = 2 * j + h
                field[0, c, t + 1, 8 : ROWS + 8, :] = field[0, c, t + 1, 8 : ROWS + 8, :] * mask
                add = (
                    fed[c * ROWS : (c + 1) * ROWS, h * 128 : (h + 1) * 128]
                    + fed[(2 + c) * ROWS : (3 + c) * ROWS, h * 128 : (h + 1) * 128]
                )
                src[c, :, t] = src[c, :, t] + add.reshape(8, 8, 128)

    def residual(s, k, slot):
        lane = lax.broadcasted_iota(jnp.int32, (ROWS, 128), 1)
        t = 2 * k + 1
        mid, beside = [], []
        for c in range(2):
            tiles = [field[s, c, t + o, 8 : ROWS + 8, :] for o in (-1, 0, 1, 2)]
            right = [pltpu.roll(tiles[i], 1, 1) for i in (0, 1, 2)]
            left = [pltpu.roll(tiles[i], 127, 1) for i in (1, 2, 3)]
            for h in range(2):
                total = (
                    field[s, c, t + h, 7 : ROWS + 7, :]
                    + field[s, c, t + h, 9 : ROWS + 9, :]
                    + jnp.where(lane == 0, right[h], right[h + 1])
                    + jnp.where(lane == 127, left[h + 1], left[h])
                )
                mid.append(tiles[1 + h])
                beside.append(total)
        for h in range(2):
            d0 = diag[0, :, 2 * k + h].reshape(ROWS, 128)
            d1 = diag[1, :, 2 * k + h].reshape(ROWS, 128)
            f0, f1 = mid[h], mid[2 + h]
            s0 = src[0, :, 2 * k + h].reshape(ROWS, 128)
            s1 = src[1, :, 2 * k + h].reshape(ROWS, 128)
            r0 = s0 - (d0 * f0 - d1 * f1 - beside[h])
            r1 = s1 - (d0 * f1 + d1 * f0 - beside[2 + h])
            for d, r in enumerate((r0, r1)):
                q = 2 * h + d
                top = r.astype(BF)
                lhs[slot, 0:ROWS, q * 128 : (q + 1) * 128] = top
                lhs[slot, ROWS : 2 * ROWS, q * 128 : (q + 1) * 128] = (r - top.astype(F32)).astype(BF)

    def relax(s, k, slot):
        both = lhs[slot]
        p = jnp.dot(both, upper[k], preferred_element_type=F32)
        q = jnp.dot(both[:ROWS], lower[k], preferred_element_type=F32)
        z = p[:ROWS] + p[ROWS:] + q
        mask = line_mask()
        for c in range(2):
            for h in range(2):
                t = 2 * k + 1 + h
                a = c * 256 + h * 128
                field[s + 1, c, t, 8 : ROWS + 8, :] = mask * (
                    field[s, c, t, 8 : ROWS + 8, :] + z[:, a : a + 128]
                )

    def send_edges(s, k):
        @pl.when((s < 3) & has_up)
        def _():
            edge_copy(0, s, k).start()

        @pl.when((s < 3) & has_down)
        def _():
            edge_copy(1, s, k).start()

    def await_edges(s, k):
        @pl.when((s > 0) & has_down)
        def _():
            edge_copy(0, s, k).wait_recv()

        @pl.when((s > 0) & has_up)
        def _():
            edge_copy(1, s, k).wait_recv()

    def out_copy(k, c, h):
        t = 2 * k + h
        return pltpu.make_async_copy(
            field.at[3, c, t + 1, pl.ds(8, ROWS), :],
            out_hbm.at[0, c, :, pl.ds(pl.multiple_of(t * 128, 128), 128)],
            o_sem.at[k, 2 * c + h],
        )

    def store_out(s, k):
        @pl.when(s == 2)
        def _():
            for c in range(2):
                for h in range(2):
                    out_copy(k, c, h).start()

    def column(which):
        lane = lax.broadcasted_iota(jnp.int32, (ROWS, 16), 1)
        return jnp.sum(jnp.where(lane == which, peers[...], 0.0), axis=1, keepdims=True)

    await_inputs(0)
    split(0)

    pl.semaphore_wait(barrier, 8 + has_up.astype(jnp.int32) + has_down.astype(jnp.int32))

    @pl.when(has_up)
    def _():
        first_edge(0).start()

    @pl.when(has_down)
    def _():
        first_edge(1).start()

    for offset in range(1, 8):
        spread(mult_hbm.at[0], held, s1_sem, r1_sem, offset, place).start()

    @pl.loop(1, EARLY)
    def _(j):
        await_inputs(j)
        split(j)

    @pl.loop(0, EARLY)
    def _(j):
        prepare(j)

    own_mult.wait()
    for c in range(2):
        src[c, :, 0] = src[c, :, 0] - held[place, c].reshape(8, 8, 128)

    @pl.when(has_down)
    def _():
        first_edge(0).wait_recv()
        scale = jnp.where(first_row + ROWS < active, 1.0, 0.0)
        for c in range(2):
            field[0, c, 1 : 2 * NB + 1, ROWS + 8 : ROWS + 9, :] = (
                field[0, c, 1 : 2 * NB + 1, ROWS + 8 : ROWS + 9, :] * scale
            )

    @pl.when(has_up)
    def _():
        first_edge(1).wait_recv()
        scale = jnp.where(first_row - 1 < active, 1.0, 0.0)
        for c in range(2):
            field[0, c, 1 : 2 * NB + 1, 7:8, :] = field[0, c, 1 : 2 * NB + 1, 7:8, :] * scale

    residual(0, 0, 0)

    @pl.loop(0, NB - EARLY)
    def _(e):
        @pl.when(e + EARLY + AHEAD < NB)
        def _():
            issue(e + EARLY + AHEAD)

        await_inputs(e + EARLY)
        slot = lax.rem(e, 2)
        split(e + EARLY)
        residual(0, e + 1, 1 - slot)
        relax(0, e, slot)
        prepare(e + EARLY)
        send_edges(1, e)

    @pl.loop(NB - EARLY, TOTAL - 1)
    def _(e):
        s, k = entry_of(e)
        s2, k2 = entry_of(e + 1)

        @pl.when(e + 1 == AT_INFLOW - 3)
        def _():
            for offset in range(1, 8):
                j = lax.rem(place + offset, places)
                spread(mult_hbm.at[0], held, s1_sem, r1_sem, offset, j).wait_recv()
            inflow[...] = jnp.zeros_like(inflow)
            part[...] = jnp.zeros_like(part)

            @pl.loop(0, 8)
            def _(j):
                seen = column(2 * j + core)
                mine = seen == sub.astype(F32)
                theirs = seen == partner.astype(F32)
                for c in range(2):
                    v = held[j, c]
                    inflow[c] = inflow[c] + jnp.where(mine, v, 0.0)
                    part[0, c] = part[0, c] + jnp.where(theirs, v, 0.0)

            to_partner(part.at[0], part_in, 0).start()

        @pl.when(e + 1 == AT_INFLOW)
        def _():
            to_partner(part.at[0], part_in, 0).wait_recv()
            for c in range(2):
                total = inflow[c] + part_in[c]
                src[c, :, 2 * NB - 1] = src[c, :, 2 * NB - 1] + total.reshape(8, 8, 128)

        await_edges(s2, k2)
        slot = lax.rem(e, 2)
        residual(s2, k2, 1 - slot)
        relax(s, k, slot)
        send_edges(s + 1, k)
        store_out(s, k)

        @pl.when(e == AT_FAR)
        def _():
            for offset in range(1, 8):
                spread(far_source(), far, s2_sem, r2_sem, offset, place).start()

    s, k = ORDER[-1]
    relax(s, k, (TOTAL - 1) % 2)
    for c in range(2):
        for h in range(2):
            out_copy(k, c, h).start()

    own_peer = column(sub)
    their_peer = column(partner)
    far[place] = field[3, :, 2 * NB, 8 : ROWS + 8, :]
    for offset in range(1, 8):
        j = lax.rem(place + offset, places)
        spread(far_source(), far, s2_sem, r2_sem, offset, j).wait_recv()
    for c in range(2):
        mine = jnp.zeros((ROWS, 128), F32)
        theirs = jnp.zeros((ROWS, 128), F32)
        for j in range(8):
            v = far[j, c]
            at = (2 * j + core).astype(F32)
            mine = mine + jnp.where(own_peer == at, v, 0.0)
            theirs = theirs + jnp.where(their_peer == at, v, 0.0)
        inflow[c] = mine
        part[1, c] = theirs
    to_partner(part.at[1], end_in, 1).start()
    to_partner(part.at[1], end_in, 1).wait_recv()
    for c in range(2):
        ahead_out[c] = held[place, c] + (field[3, c, 1, 8 : ROWS + 8, :] - (inflow[c] + end_in[c]))
    last = pltpu.make_async_copy(ahead_out, next_hbm.at[0], n_sem)
    last.start()

    @pl.when(has_up)
    def _():
        first_edge(0).wait_send()

    @pl.when(has_down)
    def _():
        first_edge(1).wait_send()

    for offset in range(1, 8):
        spread(mult_hbm.at[0], held, s1_sem, r1_sem, offset, place).wait_send()
        spread(far_source(), far, s2_sem, r2_sem, offset, place).wait_send()
    to_partner(part.at[0], part_in, 0).wait_send()
    to_partner(part.at[1], end_in, 1).wait_send()

    @pl.loop(0, NB)
    def _(k):
        for s in (1, 2):
            @pl.when(has_up)
            def _():
                edge_copy(0, s, k).wait_send()

            @pl.when(has_down)
            def _():
                edge_copy(1, s, k).wait_send()

        for c in range(2):
            for h in range(2):
                out_copy(k, c, h).wait()

    last.wait()


def per_device(
    load_current, diagonal, start_field, block_inverse, multipliers, active_rows,
    contact_peer, contact_len, port_row, port_col, port_current,
):
    width = load_current.shape[3]

    def tiled(x):
        return x.reshape(2, 8, 8, width // 128, 128).transpose(0, 1, 3, 2, 4)

    blocks = (
        block_inverse.reshape(NB, 2, 256, 2, 2, 128).transpose(0, 1, 2, 4, 3, 5).reshape(NB, 2048, 128)
    )
    hbm = pl.BlockSpec(memory_space=pl.ANY)
    dma = pltpu.SemaphoreType.DMA
    return pl.pallas_call(
        body,
        out_shape=(
            jax.ShapeDtypeStruct(load_current.shape, F32),
            jax.ShapeDtypeStruct(multipliers.shape, F32),
        ),
        in_specs=[hbm] * 6 + [pl.BlockSpec(memory_space=pltpu.SMEM)] + [hbm] * 5,
        out_specs=(hbm, hbm),
        scratch_shapes=[
            pltpu.VMEM((4, 2, 2 * NB + 2, ROWS + 16, 128), F32),
            pltpu.VMEM((2, 8, 2 * NB, 8, 128), F32),
            pltpu.VMEM((2, 8, 2 * NB, 8, 128), F32),
            pltpu.VMEM((NB, 2048, 128), F32),
            pltpu.VMEM((NB, 512, 512), BF),
            pltpu.VMEM((NB, 512, 512), BF),
            pltpu.VMEM((2, 2 * ROWS, 512), BF),
            pltpu.VMEM((8, 2, ROWS, 128), F32),
            pltpu.VMEM((8, 2, ROWS, 128), F32),
            pltpu.VMEM((2, ROWS, 128), F32),
            pltpu.VMEM((2, 2, ROWS, 128), F32),
            pltpu.VMEM((2, ROWS, 128), F32),
            pltpu.VMEM((2, ROWS, 128), F32),
            pltpu.VMEM((2, ROWS, 128), F32),
            pltpu.VMEM((ROWS, 16), F32),
            pltpu.VMEM((8, 16), jnp.int32),
            pltpu.VMEM((8, 16), jnp.int32),
            pltpu.VMEM((1, 16), jnp.int32),
            pltpu.VMEM((1, 16), jnp.int32),
            pltpu.VMEM((2, 16), F32),
            pltpu.VMEM((4 * ROWS, 16), BF),
            dma((NB, 6)),
            dma((NB,)),
            dma((6,)),
            dma((2, 3, NB)),
            dma((2, 3, NB)),
            dma((7,)),
            dma((8,)),
            dma((7,)),
            dma((8,)),
            dma((4,)),
            dma((NB, 4)),
            dma(()),
        ],
        compiler_params=pltpu.CompilerParams(
            collective_id=0, has_side_effects=True, vmem_limit_bytes=60 * 2**20
        ),
        name="relax",
    )(
        tiled(load_current), tiled(diagonal), start_field, tiled(start_field), blocks, multipliers,
        active_rows, contact_len.T, contact_peer.T, port_row, port_col, port_current[0],
    )


def solution(mesh):
    check_order()
    in_specs = (
        P("sub", None, "tile", None),
        P("sub", None, "tile", None),
        P("sub", None, "tile", None),
        P("sub", None, None, None, None, None),
        P("sub", None, "tile", None),
        P(),
        P(),
        P(),
        P("sub", None),
        P("sub", None),
        P("sub", None, None),
    )
    out_specs = (P("sub", None, "tile", None), P("sub", None, "tile", None))
    return jax.shard_map(
        per_device, mesh=mesh, in_specs=in_specs, out_specs=out_specs, check_vma=False
    )
```

profile of v0, /device:TPU:1, one launch (start us, length us, event | category | flops | bytes accessed | tf_op | source)
XLA Modules:
  0.0 52.4 jit_solution(3655599936474437267)
XLA Ops:
  0.6 48.0 %relax.1 = (f32[1,2,64,4096]{3,2,1,0:T(8,128)}, f32[1,2,64,128]{3,2,1,0:T(8,128)}) custom-call(f32[2,8,32,8,128]{4,3,2,1,0:T(8,128)} %bitcast.19, f32[2,8,32,8,128]{4,3,2,1,0:T(8,128)} %bitcast.20, f32[1,2,64,4096]{3,2,1,0:T(8,128)} %start_hbm.1, f32[2,8,32,8,128]{4,3,2,1,0:T(8,128)} %bitcast.18, f32[16,2048,128]{2,1,0:T(8,128)} %bitcast.17, ...), custom_call_target="tpu_custom_call" | custom-call | tf_op jit(solution)/shard_map/relax/pallas_call | solution.py:522
  48.6 0.0 copy-start
  48.7 3.1 %copy.16 = f32[1,2,64,4096]{3,2,1,0:T(8,128)} copy(f32[1,2,64,4096]{3,2,1,0:T(8,128)} %get-tuple-element.4) | data formatting | bytes 4194304
  51.8 0.0 copy-done
  51.8 0.6 %copy.17 = f32[1,2,64,128]{3,2,1,0:T(8,128)} copy(f32[1,2,64,128]{3,2,1,0:T(8,128)S(1)} %copy-done) | data formatting | bytes 131072
Async XLA Ops:
  48.6 3.2 %copy-start = (f32[1,2,64,128]{3,2,1,0:T(8,128)S(1)}, f32[1,2,64,128]{3,2,1,0:T(8,128)}, u32[]{:S(2)}) copy-start(f32[1,2,64,128]{3,2,1,0:T(8,128)} %get-tuple-element.5) | copy-start | bytes 196612
where the time goes:
time: 53.5 us; the launch traced here: 52.4 us
  Pallas kernels  48 us (90%)
  local copies, waits for them, and re-layouts  3.78 us (7%)
  between operations  0.65 us (1%)
    pallas_call x1, Pallas kernels, per_device(): pl.pallas_call(body, out_shape=(jax.ShapeDtypeStruct(load_current.shape,...  48 us
    unnamed x4, local copies, waits for them, and re-layouts  3.78 us

commit v1 on v0

--- a/solution.py
+++ b/solution.py
@@ -13,18 +13,16 @@
 NB = 16
 ROWS = 64
 EARLY = 5
-AHEAD = 4
 
 RUNS = (
     (0, 0, 1, 15),
-    (1, 0, 1, 11),
+    (1, 0, 1, 3),
     (0, 15, 1, 1),
-    (1, 11, 1, 2),
-    (2, 0, 1, 4),
+    (1, 3, 1, 6),
     (1, 15, -1, 3),
-    (2, 4, 1, 4),
+    (1, 9, 1, 4),
     (2, 15, 1, 1),
-    (2, 8, 1, 7),
+    (2, 0, 1, 15),
 )
 ORDER = [(s, k0 + d * i) for s, k0, d, n in RUNS for i in range(n)]
 TOTAL = len(ORDER)
@@ -55,13 +53,13 @@
 
 
 def body(
-    load_hbm, diag_hbm, start_hbm, edge_hbm, block_hbm, mult_hbm, active_ref,
+    load_hbm, diag_hbm, start_hbm, edge_hbm, block_hbm, mult_hbm, active_hbm,
     len_hbm, peer_hbm, prow_hbm, pcol_hbm, pcur_hbm,
-    out_hbm, next_hbm,
+    out_ref, next_ref,
     field, src, diag, stage, upper, lower, lhs,
-    held, far, inflow, part, part_in, end_in, ahead_out,
-    peers, lens, cpeer, prow, pcol, pcur, weights,
-    in_sem, b_sem, small_sem, hs_sem, hr_sem, s1_sem, r1_sem, s2_sem, r2_sem, p_sem, o_sem, n_sem,
+    held, far, inflow, part, part_in, end_in,
+    peers, lens, cpeer, prow, pcol, pcur, weights, active_ref,
+    in_sem, b_sem, small_sem, hs_sem, hr_sem, s1_sem, r1_sem, s2_sem, r2_sem, p_sem,
 ):
     sub = lax.axis_index("sub")
     tile = lax.axis_index("tile")
@@ -71,8 +69,10 @@
     places = lax.axis_size("sub") // 2
     partner = place * 2 + (1 - core)
     first_row = tile * ROWS
-    has_up = tile > 0
-    has_down = tile < last_tile
+    above = lax.rem(tile + last_tile, last_tile + 1)
+    below = lax.rem(tile + 1, last_tile + 1)
+    line_above = jnp.where(tile > 0, ROWS + 8, ROWS + 9)
+    line_below = jnp.where(tile < last_tile, 7, 6)
 
     def inputs_of(j):
         t = 2 * j
@@ -111,30 +111,30 @@
         for i, (a, b) in enumerate(
             (
                 (len_hbm, lens), (peer_hbm, cpeer), (prow_hbm, prow),
-                (pcol_hbm, pcol), (pcur_hbm, pcur),
+                (pcol_hbm, pcol), (pcur_hbm, pcur), (active_hbm, active_ref),
             )
         )
     ]
-    own_mult = pltpu.make_async_copy(mult_hbm.at[0], held.at[place], small_sem.at[5])
+    own_mult = pltpu.make_async_copy(mult_hbm.at[0], held.at[place], small_sem.at[6])
 
     def edge_copy(side, s, k):
         t = 2 * k + 1
-        row, there, to = ((8, ROWS + 8, tile - 1), (ROWS + 7, 7, tile + 1))[side]
+        row, there, to = ((8, line_above, above), (ROWS + 7, line_below, below))[side]
         return pltpu.make_async_remote_copy(
             src_ref=field.at[s, :, pl.ds(t, 2), pl.ds(row, 1), :],
             dst_ref=field.at[s, :, pl.ds(t, 2), pl.ds(there, 1), :],
-            send_sem=hs_sem.at[side, s, k],
+            send_sem=hs_sem.at[side, s],
             recv_sem=hr_sem.at[side, s, k],
             device_id=(sub, to),
             device_id_type=MESH,
         )
 
     def first_edge(side):
-        group, line, there, to = ((0, 0, ROWS + 8, tile - 1), (7, 7, 7, tile + 1))[side]
+        group, line, there, to = ((0, 0, line_above, above), (7, 7, line_below, below))[side]
         return pltpu.make_async_remote_copy(
             src_ref=edge_hbm.at[:, group, :, pl.ds(line, 1), :],
             dst_ref=field.at[0, :, pl.ds(1, 2 * NB), pl.ds(there, 1), :],
-            send_sem=hs_sem.at[side, 0, 0],
+            send_sem=hs_sem.at[side, 0],
             recv_sem=hr_sem.at[side, 0, 0],
             device_id=(sub, to),
             device_id_type=MESH,
@@ -162,7 +162,7 @@
         )
 
     def far_source():
-        return field.at[3, :, 2 * NB, pl.ds(8, ROWS), :]
+        return out_ref.at[:, :, 2 * NB - 1]
 
     for copy in small:
         copy.start()
@@ -175,15 +175,11 @@
         pl.semaphore_signal(barrier, inc=1, device_id=(to * 2 + core, tile), device_id_type=MESH)
     pl.semaphore_signal(barrier, inc=1, device_id=(partner, tile), device_id_type=MESH)
 
-    @pl.when(has_up)
-    def _():
-        pl.semaphore_signal(barrier, inc=1, device_id=(sub, tile - 1), device_id_type=MESH)
-
-    @pl.when(has_down)
-    def _():
-        pl.semaphore_signal(barrier, inc=1, device_id=(sub, tile + 1), device_id_type=MESH)
-
-    for j in range(2, EARLY + AHEAD):
+    pl.semaphore_signal(barrier, inc=1, device_id=(sub, above), device_id_type=MESH)
+    pl.semaphore_signal(barrier, inc=1, device_id=(sub, below), device_id_type=MESH)
+
+    @pl.loop(2, NB)
+    def _(j):
         issue(j)
 
     for s in range(3):
@@ -288,52 +284,43 @@
                 lhs[slot, 0:ROWS, q * 128 : (q + 1) * 128] = top
                 lhs[slot, ROWS : 2 * ROWS, q * 128 : (q + 1) * 128] = (r - top.astype(F32)).astype(BF)
 
-    def relax(s, k, slot):
+    def relax(s, k, slot, final=None):
         both = lhs[slot]
         p = jnp.dot(both, upper[k], preferred_element_type=F32)
         q = jnp.dot(both[:ROWS], lower[k], preferred_element_type=F32)
         z = p[:ROWS] + p[ROWS:] + q
         mask = line_mask()
+        fresh = []
         for c in range(2):
             for h in range(2):
-                t = 2 * k + 1 + h
                 a = c * 256 + h * 128
-                field[s + 1, c, t, 8 : ROWS + 8, :] = mask * (
-                    field[s, c, t, 8 : ROWS + 8, :] + z[:, a : a + 128]
-                )
-
-    def send_edges(s, k):
-        @pl.when((s < 3) & has_up)
-        def _():
-            edge_copy(0, s, k).start()
-
-        @pl.when((s < 3) & has_down)
-        def _():
-            edge_copy(1, s, k).start()
-
-    def await_edges(s, k):
-        @pl.when((s > 0) & has_down)
-        def _():
-            edge_copy(0, s, k).wait_recv()
-
-        @pl.when((s > 0) & has_up)
-        def _():
-            edge_copy(1, s, k).wait_recv()
-
-    def out_copy(k, c, h):
-        t = 2 * k + h
-        return pltpu.make_async_copy(
-            field.at[3, c, t + 1, pl.ds(8, ROWS), :],
-            out_hbm.at[0, c, :, pl.ds(pl.multiple_of(t * 128, 128), 128)],
-            o_sem.at[k, 2 * c + h],
-        )
-
-    def store_out(s, k):
-        @pl.when(s == 2)
-        def _():
+                fresh.append(mask * (field[s, c, 2 * k + 1 + h, 8 : ROWS + 8, :] + z[:, a : a + 128]))
+
+        def keep():
             for c in range(2):
                 for h in range(2):
-                    out_copy(k, c, h).start()
+                    field[s + 1, c, 2 * k + 1 + h, 8 : ROWS + 8, :] = fresh[2 * c + h]
+
+        def give():
+            for c in range(2):
+                for h in range(2):
+                    out_ref[c, :, 2 * k + h] = fresh[2 * c + h].reshape(8, 8, 128)
+
+        if final is None:
+            pl.when(s < 2)(keep)
+            pl.when(s == 2)(give)
+        elif final:
+            give()
+        else:
+            keep()
+
+    def send_edges(s, k):
+        edge_copy(0, s, k).start()
+        edge_copy(1, s, k).start()
+
+    def await_edges(s, k):
+        edge_copy(0, s, k).wait_recv()
+        edge_copy(1, s, k).wait_recv()
 
     def column(which):
         lane = lax.broadcasted_iota(jnp.int32, (ROWS, 16), 1)
@@ -342,15 +329,9 @@
     await_inputs(0)
     split(0)
 
-    pl.semaphore_wait(barrier, 8 + has_up.astype(jnp.int32) + has_down.astype(jnp.int32))
-
-    @pl.when(has_up)
-    def _():
-        first_edge(0).start()
-
-    @pl.when(has_down)
-    def _():
-        first_edge(1).start()
+    pl.semaphore_wait(barrier, 10)
+    first_edge(0).start()
+    first_edge(1).start()
 
     for offset in range(1, 8):
         spread(mult_hbm.at[0], held, s1_sem, r1_sem, offset, place).start()
@@ -368,42 +349,28 @@
     for c in range(2):
         src[c, :, 0] = src[c, :, 0] - held[place, c].reshape(8, 8, 128)
 
-    @pl.when(has_down)
-    def _():
-        first_edge(0).wait_recv()
-        scale = jnp.where(first_row + ROWS < active, 1.0, 0.0)
+    for side, row, line in ((0, ROWS + 8, first_row + ROWS), (1, 7, first_row - 1)):
+        first_edge(side).wait_recv()
+        scale = jnp.where(line < active, 1.0, 0.0)
         for c in range(2):
-            field[0, c, 1 : 2 * NB + 1, ROWS + 8 : ROWS + 9, :] = (
-                field[0, c, 1 : 2 * NB + 1, ROWS + 8 : ROWS + 9, :] * scale
+            field[0, c, 1 : 2 * NB + 1, row : row + 1, :] = (
+                field[0, c, 1 : 2 * NB + 1, row : row + 1, :] * scale
             )
-
-    @pl.when(has_up)
-    def _():
-        first_edge(1).wait_recv()
-        scale = jnp.where(first_row - 1 < active, 1.0, 0.0)
-        for c in range(2):
-            field[0, c, 1 : 2 * NB + 1, 7:8, :] = field[0, c, 1 : 2 * NB + 1, 7:8, :] * scale
 
     residual(0, 0, 0)
 
     @pl.loop(0, NB - EARLY)
     def _(e):
-        @pl.when(e + EARLY + AHEAD < NB)
-        def _():
-            issue(e + EARLY + AHEAD)
-
         await_inputs(e + EARLY)
         slot = lax.rem(e, 2)
         split(e + EARLY)
         residual(0, e + 1, 1 - slot)
-        relax(0, e, slot)
+        relax(0, e, slot, False)
         prepare(e + EARLY)
         send_edges(1, e)
 
-    @pl.loop(NB - EARLY, TOTAL - 1)
-    def _(e):
-        s, k = entry_of(e)
-        s2, k2 = entry_of(e + 1)
+    def later(e, carry):
+        s, k, s2, k2 = carry
 
         @pl.when(e + 1 == AT_INFLOW - 3)
         def _():
@@ -432,27 +399,34 @@
                 total = inflow[c] + part_in[c]
                 src[c, :, 2 * NB - 1] = src[c, :, 2 * NB - 1] + total.reshape(8, 8, 128)
 
-        await_edges(s2, k2)
+        @pl.when(s2 > 0)
+        def _():
+            await_edges(s2, k2)
+
         slot = lax.rem(e, 2)
+        s3, k3 = entry_of(e + 2)
         residual(s2, k2, 1 - slot)
         relax(s, k, slot)
-        send_edges(s + 1, k)
-        store_out(s, k)
+
+        @pl.when(s < 2)
+        def _():
+            send_edges(s + 1, k)
 
         @pl.when(e == AT_FAR)
         def _():
             for offset in range(1, 8):
                 spread(far_source(), far, s2_sem, r2_sem, offset, place).start()
 
+        return s2, k2, s3, k3
+
+    first = NB - EARLY
+    lax.fori_loop(first, TOTAL - 1, later, (*entry_of(jnp.int32(first)), *entry_of(jnp.int32(first + 1))))
     s, k = ORDER[-1]
-    relax(s, k, (TOTAL - 1) % 2)
-    for c in range(2):
-        for h in range(2):
-            out_copy(k, c, h).start()
+    relax(s, k, (TOTAL - 1) % 2, True)
 
     own_peer = column(sub)
     their_peer = column(partner)
-    far[place] = field[3, :, 2 * NB, 8 : ROWS + 8, :]
+    far[place] = out_ref[:, :, 2 * NB - 1]
     for offset in range(1, 8):
         j = lax.rem(place + offset, places)
         spread(far_source(), far, s2_sem, r2_sem, offset, j).wait_recv()
@@ -460,7 +434,7 @@
         mine = jnp.zeros((ROWS, 128), F32)
         theirs = jnp.zeros((ROWS, 128), F32)
         for j in range(8):
-            v = far[j, c]
+            v = far[j, c].reshape(ROWS, 128)
             at = (2 * j + core).astype(F32)
             mine = mine + jnp.where(own_peer == at, v, 0.0)
             theirs = theirs + jnp.where(their_peer == at, v, 0.0)
@@ -469,17 +443,8 @@
     to_partner(part.at[1], end_in, 1).start()
     to_partner(part.at[1], end_in, 1).wait_recv()
     for c in range(2):
-        ahead_out[c] = held[place, c] + (field[3, c, 1, 8 : ROWS + 8, :] - (inflow[c] + end_in[c]))
-    last = pltpu.make_async_copy(ahead_out, next_hbm.at[0], n_sem)
-    last.start()
-
-    @pl.when(has_up)
-    def _():
-        first_edge(0).wait_send()
-
-    @pl.when(has_down)
-    def _():
-        first_edge(1).wait_send()
+        near = out_ref[c, :, 0].reshape(ROWS, 128)
+        next_ref[0, c] = held[place, c] + (near - (inflow[c] + end_in[c]))
 
     for offset in range(1, 8):
         spread(mult_hbm.at[0], held, s1_sem, r1_sem, offset, place).wait_send()
@@ -487,22 +452,18 @@
     to_partner(part.at[0], part_in, 0).wait_send()
     to_partner(part.at[1], end_in, 1).wait_send()
 
-    @pl.loop(0, NB)
-    def _(k):
+    for side in range(2):
+        first_edge(side).wait_send()
+        row, there, to = ((8, line_above, above), (ROWS + 7, line_below, below))[side]
         for s in (1, 2):
-            @pl.when(has_up)
-            def _():
-                edge_copy(0, s, k).wait_send()
-
-            @pl.when(has_down)
-            def _():
-                edge_copy(1, s, k).wait_send()
-
-        for c in range(2):
-            for h in range(2):
-                out_copy(k, c, h).wait()
-
-    last.wait()
+            pltpu.make_async_remote_copy(
+                src_ref=field.at[s, :, pl.ds(1, 2 * NB), pl.ds(row, 1), :],
+                dst_ref=field.at[s, :, pl.ds(1, 2 * NB), pl.ds(there, 1), :],
+                send_sem=hs_sem.at[side, s],
+                recv_sem=hr_sem.at[side, s, 0],
+                device_id=(sub, to),
+                device_id_type=MESH,
+            ).wait_send()
 
 
 def per_device(
@@ -514,21 +475,25 @@
     def tiled(x):
         return x.reshape(2, 8, 8, width // 128, 128).transpose(0, 1, 3, 2, 4)
 
+    def stay(x):
+        return pltpu.with_memory_space_constraint(x, pltpu.HBM)
+
     blocks = (
         block_inverse.reshape(NB, 2, 256, 2, 2, 128).transpose(0, 1, 2, 4, 3, 5).reshape(NB, 2048, 128)
     )
-    hbm = pl.BlockSpec(memory_space=pl.ANY)
+    hbm = pl.BlockSpec(memory_space=pltpu.HBM)
+    vmem = pl.BlockSpec(memory_space=pltpu.VMEM)
     dma = pltpu.SemaphoreType.DMA
-    return pl.pallas_call(
+    solved, following = pl.pallas_call(
         body,
         out_shape=(
-            jax.ShapeDtypeStruct(load_current.shape, F32),
+            jax.ShapeDtypeStruct((2, 8, 2 * NB, 8, 128), F32),
             jax.ShapeDtypeStruct(multipliers.shape, F32),
         ),
-        in_specs=[hbm] * 6 + [pl.BlockSpec(memory_space=pltpu.SMEM)] + [hbm] * 5,
-        out_specs=(hbm, hbm),
+        in_specs=[hbm] * 12,
+        out_specs=(vmem, vmem),
         scratch_shapes=[
-            pltpu.VMEM((4, 2, 2 * NB + 2, ROWS + 16, 128), F32),
+            pltpu.VMEM((3, 2, 2 * NB + 2, ROWS + 16, 128), F32),
             pltpu.VMEM((2, 8, 2 * NB, 8, 128), F32),
             pltpu.VMEM((2, 8, 2 * NB, 8, 128), F32),
             pltpu.VMEM((NB, 2048, 128), F32),
@@ -536,10 +501,9 @@
             pltpu.VMEM((NB, 512, 512), BF),
             pltpu.VMEM((2, 2 * ROWS, 512), BF),
             pltpu.VMEM((8, 2, ROWS, 128), F32),
-            pltpu.VMEM((8, 2, ROWS, 128), F32),
+            pltpu.VMEM((8, 2, 8, 8, 128), F32),
             pltpu.VMEM((2, ROWS, 128), F32),
             pltpu.VMEM((2, 2, ROWS, 128), F32),
-            pltpu.VMEM((2, ROWS, 128), F32),
             pltpu.VMEM((2, ROWS, 128), F32),
             pltpu.VMEM((2, ROWS, 128), F32),
             pltpu.VMEM((ROWS, 16), F32),
@@ -549,27 +513,28 @@
             pltpu.VMEM((1, 16), jnp.int32),
             pltpu.VMEM((2, 16), F32),
             pltpu.VMEM((4 * ROWS, 16), BF),
+            pltpu.SMEM((16,), jnp.int32),
             dma((NB, 6)),
             dma((NB,)),
-            dma((6,)),
-            dma((2, 3, NB)),
+            dma((7,)),
+            dma((2, 3)),
             dma((2, 3, NB)),
             dma((7,)),
             dma((8,)),
             dma((7,)),
             dma((8,)),
             dma((4,)),
-            dma((NB, 4)),
-            dma(()),
         ],
         compiler_params=pltpu.CompilerParams(
-            collective_id=0, has_side_effects=True, vmem_limit_bytes=60 * 2**20
+            collective_id=0, has_side_effects=True, vmem_limit_bytes=51 * 2**20
         ),
         name="relax",
     )(
-        tiled(load_current), tiled(diagonal), start_field, tiled(start_field), blocks, multipliers,
-        active_rows, contact_len.T, contact_peer.T, port_row, port_col, port_current[0],
+        tiled(load_current), tiled(diagonal), start_field, tiled(start_field), blocks, stay(multipliers),
+        stay(active_rows), stay(contact_len.T), stay(contact_peer.T), stay(port_row), stay(port_col),
+        stay(port_current[0]),
     )
+    return solved.transpose(0, 1, 3, 2, 4).reshape(load_current.shape), following
 
 
 def solution(mesh):

time: 53.5 us -> 46.2 us (0.86); the launches traced: 52.4 us -> 46.1 us
  Pallas kernels: 48 us -> 43.5 us
  local copies, waits for them, and re-layouts: 3.78 us -> 1.95 us
    pallas_call x1, Pallas kernels: 48 us -> 43.5 us  [per_device(): pl.pallas_call(body, out_shape=(jax.ShapeDtypeStruct((2, 8, 2 * NB, 8, 12...]
    unnamed x4 -> x2, local copies, waits for them, and re-layouts: 3.78 us -> 1.95 us
where the time goes in v1:
time: 46.2 us; the launch traced here: 46.1 us
  Pallas kernels  43.5 us (94%)
  local copies, waits for them, and re-layouts  1.95 us (4%)
  between operations  0.64 us (1%)
    pallas_call x1, Pallas kernels, per_device(): pl.pallas_call(body, out_shape=(jax.ShapeDtypeStruct((2, 8, 2 * NB, 8, 12...  43.5 us
    unnamed x2, local copies, waits for them, and re-layouts  1.95 us

profile of v1, /device:TPU:1, one launch (start us, length us, event | category | flops | bytes accessed | tf_op | source)
XLA Modules:
  0.0 46.1 jit_solution(11369039167736991091)
XLA Ops:
  0.6 43.5 %relax.1 = (f32[2,8,32,8,128]{4,3,2,1,0:T(8,128)S(1)}, f32[1,2,64,128]{3,2,1,0:T(8,128)S(1)}) custom-call(f32[2,8,32,8,128]{4,3,2,1,0:T(8,128)} %bitcast.23, f32[2,8,32,8,128]{4,3,2,1,0:T(8,128)} %bitcast.24, f32[1,2,64,4096]{3,2,1,0:T(8,128)} %start_hbm.1, f32[2,8,32,8,128]{4,3,2,1,0:T(8,128)} %bitcast.22, f32[16,2048,128]{2,1,0:T(8,128)} %bitcast.21, ...), custom_call_target="tpu_custom_call" | custom-call | tf_op jit(solution)/shard_map/relax/pallas_call | solution.py:487
  44.1 1.3 %copy.16 = f32[1,2,64,4096]{3,2,1,0:T(8,128)} copy(f32[1,2,64,4096]{3,2,1,0:T(8,128)S(1)} %bitcast.20) | data formatting | bytes 4194304
  45.4 0.6 %copy.17 = f32[1,2,64,128]{3,2,1,0:T(8,128)} copy(f32[1,2,64,128]{3,2,1,0:T(8,128)S(1)} %get-tuple-element.9) | data formatting | bytes 131072

commit v2 on v1

--- a/solution.py
+++ b/solution.py
@@ -12,43 +12,46 @@
 F32 = jnp.float32
 NB = 16
 ROWS = 64
-EARLY = 5
-
-RUNS = (
-    (0, 0, 1, 15),
-    (1, 0, 1, 3),
-    (0, 15, 1, 1),
-    (1, 3, 1, 6),
-    (1, 15, -1, 3),
-    (1, 9, 1, 4),
-    (2, 15, 1, 1),
-    (2, 0, 1, 15),
+EARLY = 4
+
+EVEN = ((0, 0, 0, 2), (8, 1, 0, 2), (12, 1, 14, 0), (13, 1, 8, 2), (16, 2, 0, 2))
+ODD = (
+    (0, 0, 1, 2), (7, 1, 1, 0), (8, 0, 15, 0), (9, 1, 3, 2), (12, 1, 15, 0),
+    (13, 1, 9, 2), (16, 2, 15, 0), (17, 2, 1, 2),
 )
-ORDER = [(s, k0 + d * i) for s, k0, d, n in RUNS for i in range(n)]
-TOTAL = len(ORDER)
-AT = {entry: e for e, entry in enumerate(ORDER)}
-AT_INFLOW = AT[(0, 15)]
-AT_FAR = AT[(2, 15)]
+STEPS = 24
+SPLITS = (NB - EARLY) // 2
+AT_INFLOW = 8
+AT_FAR = 16
+
+
+def static_entry(runs, m):
+    first, s, k0, d = [run for run in runs if run[0] <= m][-1]
+    return s, k0 + d * (m - first)
 
 
 def check_order():
-    assert sorted(ORDER) == [(s, k) for s in range(3) for k in range(NB)]
-    for s, k in ORDER:
+    order = [static_entry(r, m) for m in range(STEPS) for r in (EVEN, ODD)]
+    at = {entry: e for e, entry in enumerate(order)}
+    assert sorted(order) == [(s, k) for s in range(3) for k in range(NB)]
+    assert order[2 * AT_INFLOW + 1] == (0, 15) and order[2 * AT_FAR + 1] == (2, 15)
+    assert all(k % 2 == e % 2 for e, (s, k) in enumerate(order))
+    assert all(order[e] == (0, e) for e in range(2 * SPLITS + 1))
+    for s, k in order:
         if s:
             for j in (k - 1, k, k + 1):
                 if 0 <= j < NB:
-                    assert AT[(s - 1, j)] + 2 <= AT[(s, k)]
-
-
-def entry_of(e):
-    sweep = jnp.int32(RUNS[0][0])
-    block = RUNS[0][1] + RUNS[0][2] * e
-    start = RUNS[0][3]
-    for s, k0, d, n in RUNS[1:]:
-        later = e >= start
+                    assert at[(s - 1, j)] + 2 <= at[(s, k)]
+
+
+def entry_of(runs, m):
+    _, s, k0, d = runs[0]
+    sweep = jnp.int32(s)
+    block = k0 + d * m
+    for first, s, k0, d in runs[1:]:
+        later = m >= first
         sweep = jnp.where(later, s, sweep)
-        block = jnp.where(later, k0 + d * (e - start), block)
-        start += n
+        block = jnp.where(later, k0 + d * (m - first), block)
     return sweep, block
 
 
@@ -56,7 +59,7 @@
     load_hbm, diag_hbm, start_hbm, edge_hbm, block_hbm, mult_hbm, active_hbm,
     len_hbm, peer_hbm, prow_hbm, pcol_hbm, pcur_hbm,
     out_ref, next_ref,
-    field, src, diag, stage, upper, lower, lhs,
+    field, src, diag, stage, upper_even, lower_even, upper_odd, lower_odd, lhs_even, lhs_odd,
     held, far, inflow, part, part_in, end_in,
     peers, lens, cpeer, prow, pcol, pcur, weights, active_ref,
     in_sem, b_sem, small_sem, hs_sem, hr_sem, s1_sem, r1_sem, s2_sem, r2_sem, p_sem,
@@ -162,7 +165,7 @@
         )
 
     def far_source():
-        return out_ref.at[:, :, 2 * NB - 1]
+        return field.at[3, :, 2 * NB, pl.ds(8, ROWS), :]
 
     for copy in small:
         copy.start()
@@ -226,12 +229,13 @@
         line = lax.broadcasted_iota(jnp.int32, (ROWS, 128), 0) + first_row
         return (line < active).astype(F32)
 
-    def split(j):
+    def split(j, odd):
+        upper, lower = ((upper_even, lower_even), (upper_odd, lower_odd))[odd]
         for q in range(4):
             v = stage[j, pl.ds(q, 512, stride=4), :].T
             top = v.astype(BF)
-            upper[j, q * 128 : (q + 1) * 128, :] = top
-            lower[j, q * 128 : (q + 1) * 128, :] = (v - top.astype(F32)).astype(BF)
+            upper[j // 2, q * 128 : (q + 1) * 128, :] = top
+            lower[j // 2, q * 128 : (q + 1) * 128, :] = (v - top.astype(F32)).astype(BF)
 
     def await_inputs(j):
         for copy in inputs_of(j):
@@ -253,7 +257,7 @@
                 )
                 src[c, :, t] = src[c, :, t] + add.reshape(8, 8, 128)
 
-    def residual(s, k, slot):
+    def residual(s, k, lhs):
         lane = lax.broadcasted_iota(jnp.int32, (ROWS, 128), 1)
         t = 2 * k + 1
         mid, beside = [], []
@@ -281,38 +285,25 @@
             for d, r in enumerate((r0, r1)):
                 q = 2 * h + d
                 top = r.astype(BF)
-                lhs[slot, 0:ROWS, q * 128 : (q + 1) * 128] = top
-                lhs[slot, ROWS : 2 * ROWS, q * 128 : (q + 1) * 128] = (r - top.astype(F32)).astype(BF)
-
-    def relax(s, k, slot, final=None):
-        both = lhs[slot]
-        p = jnp.dot(both, upper[k], preferred_element_type=F32)
-        q = jnp.dot(both[:ROWS], lower[k], preferred_element_type=F32)
-        z = p[:ROWS] + p[ROWS:] + q
+                lhs[0:ROWS, q * 128 : (q + 1) * 128] = top
+                lhs[ROWS : 2 * ROWS, q * 128 : (q + 1) * 128] = (r - top.astype(F32)).astype(BF)
+
+    def product(k, odd):
+        lhs, upper, lower = ((lhs_even, upper_even, lower_even), (lhs_odd, upper_odd, lower_odd))[odd]
+        both = lhs[...]
+        p = jnp.dot(both, upper[k // 2], preferred_element_type=F32)
+        q = jnp.dot(both[:ROWS], lower[k // 2], preferred_element_type=F32)
+        return p[:ROWS] + p[ROWS:] + q
+
+    def update(s, k, z):
         mask = line_mask()
-        fresh = []
         for c in range(2):
             for h in range(2):
+                t = 2 * k + 1 + h
                 a = c * 256 + h * 128
-                fresh.append(mask * (field[s, c, 2 * k + 1 + h, 8 : ROWS + 8, :] + z[:, a : a + 128]))
-
-        def keep():
-            for c in range(2):
-                for h in range(2):
-                    field[s + 1, c, 2 * k + 1 + h, 8 : ROWS + 8, :] = fresh[2 * c + h]
-
-        def give():
-            for c in range(2):
-                for h in range(2):
-                    out_ref[c, :, 2 * k + h] = fresh[2 * c + h].reshape(8, 8, 128)
-
-        if final is None:
-            pl.when(s < 2)(keep)
-            pl.when(s == 2)(give)
-        elif final:
-            give()
-        else:
-            keep()
+                field[s + 1, c, t, 8 : ROWS + 8, :] = mask * (
+                    field[s, c, t, 8 : ROWS + 8, :] + z[:, a : a + 128]
+                )
 
     def send_edges(s, k):
         edge_copy(0, s, k).start()
@@ -327,7 +318,7 @@
         return jnp.sum(jnp.where(lane == which, peers[...], 0.0), axis=1, keepdims=True)
 
     await_inputs(0)
-    split(0)
+    split(0, 0)
 
     pl.semaphore_wait(barrier, 10)
     first_edge(0).start()
@@ -336,10 +327,9 @@
     for offset in range(1, 8):
         spread(mult_hbm.at[0], held, s1_sem, r1_sem, offset, place).start()
 
-    @pl.loop(1, EARLY)
-    def _(j):
+    for j in range(1, EARLY):
         await_inputs(j)
-        split(j)
+        split(j, j % 2)
 
     @pl.loop(0, EARLY)
     def _(j):
@@ -357,22 +347,30 @@
                 field[0, c, 1 : 2 * NB + 1, row : row + 1, :] * scale
             )
 
-    residual(0, 0, 0)
-
-    @pl.loop(0, NB - EARLY)
-    def _(e):
+    residual(0, 0, lhs_even)
+
+    @pl.loop(0, SPLITS)
+    def _(m):
+        e = 2 * m
         await_inputs(e + EARLY)
-        slot = lax.rem(e, 2)
-        split(e + EARLY)
-        residual(0, e + 1, 1 - slot)
-        relax(0, e, slot, False)
+        await_inputs(e + EARLY + 1)
+        residual(0, e + 1, lhs_odd)
+        z = product(e, 0)
+        split(e + EARLY + 1, 1)
         prepare(e + EARLY)
+        prepare(e + EARLY + 1)
+        update(0, e, z)
+        residual(0, e + 2, lhs_even)
+        z = product(e + 1, 1)
+        split(e + EARLY, 0)
+        update(0, e + 1, z)
         send_edges(1, e)
-
-    def later(e, carry):
-        s, k, s2, k2 = carry
-
-        @pl.when(e + 1 == AT_INFLOW - 3)
+        send_edges(1, e + 1)
+
+    def later(m, carry):
+        s0, k0, s1, k1, s2, k2 = carry
+
+        @pl.when(m == AT_INFLOW - 1)
         def _():
             for offset in range(1, 8):
                 j = lax.rem(place + offset, places)
@@ -392,41 +390,61 @@
 
             to_partner(part.at[0], part_in, 0).start()
 
-        @pl.when(e + 1 == AT_INFLOW)
+        @pl.when(m == AT_INFLOW)
         def _():
             to_partner(part.at[0], part_in, 0).wait_recv()
             for c in range(2):
                 total = inflow[c] + part_in[c]
                 src[c, :, 2 * NB - 1] = src[c, :, 2 * NB - 1] + total.reshape(8, 8, 128)
 
+        @pl.when(s1 > 0)
+        def _():
+            await_edges(s1, k1)
+
         @pl.when(s2 > 0)
         def _():
             await_edges(s2, k2)
 
-        slot = lax.rem(e, 2)
-        s3, k3 = entry_of(e + 2)
-        residual(s2, k2, 1 - slot)
-        relax(s, k, slot)
-
-        @pl.when(s < 2)
-        def _():
-            send_edges(s + 1, k)
-
-        @pl.when(e == AT_FAR)
+        s3, k3 = entry_of(ODD, m + 1)
+        s4, k4 = entry_of(EVEN, m + 2)
+        residual(s1, k1, lhs_odd)
+        update(s0, k0, product(k0, 0))
+        residual(s2, k2, lhs_even)
+        update(s1, k1, product(k1, 1))
+
+        @pl.when(s0 < 2)
+        def _():
+            send_edges(s0 + 1, k0)
+
+        @pl.when(s1 < 2)
+        def _():
+            send_edges(s1 + 1, k1)
+
+        @pl.when(m == AT_FAR)
         def _():
             for offset in range(1, 8):
                 spread(far_source(), far, s2_sem, r2_sem, offset, place).start()
 
-        return s2, k2, s3, k3
-
-    first = NB - EARLY
-    lax.fori_loop(first, TOTAL - 1, later, (*entry_of(jnp.int32(first)), *entry_of(jnp.int32(first + 1))))
-    s, k = ORDER[-1]
-    relax(s, k, (TOTAL - 1) % 2, True)
+        return s2, k2, s3, k3, s4, k4
+
+    first = jnp.int32(SPLITS)
+    lax.fori_loop(
+        SPLITS, STEPS - 1, later,
+        (*entry_of(EVEN, first), *entry_of(ODD, first), *entry_of(EVEN, first + 1)),
+    )
+    s, k = static_entry(ODD, STEPS - 1)
+    await_edges(s, k)
+    residual(s, k, lhs_odd)
+    s0, k0 = static_entry(EVEN, STEPS - 1)
+    update(s0, k0, product(k0, 0))
+    update(s, k, product(k, 1))
+    for c in range(2):
+        for g in range(8):
+            out_ref[c, g] = field[3, c, 1 : 2 * NB + 1, 8 * g + 8 : 8 * g + 16, :]
 
     own_peer = column(sub)
     their_peer = column(partner)
-    far[place] = out_ref[:, :, 2 * NB - 1]
+    far[place] = field[3, :, 2 * NB, 8 : ROWS + 8, :]
     for offset in range(1, 8):
         j = lax.rem(place + offset, places)
         spread(far_source(), far, s2_sem, r2_sem, offset, j).wait_recv()
@@ -434,7 +452,7 @@
         mine = jnp.zeros((ROWS, 128), F32)
         theirs = jnp.zeros((ROWS, 128), F32)
         for j in range(8):
-            v = far[j, c].reshape(ROWS, 128)
+            v = far[j, c]
             at = (2 * j + core).astype(F32)
             mine = mine + jnp.where(own_peer == at, v, 0.0)
             theirs = theirs + jnp.where(their_peer == at, v, 0.0)
@@ -443,7 +461,7 @@
     to_partner(part.at[1], end_in, 1).start()
     to_partner(part.at[1], end_in, 1).wait_recv()
     for c in range(2):
-        near = out_ref[c, :, 0].reshape(ROWS, 128)
+        near = field[3, c, 1, 8 : ROWS + 8, :]
         next_ref[0, c] = held[place, c] + (near - (inflow[c] + end_in[c]))
 
     for offset in range(1, 8):
@@ -493,15 +511,18 @@
         in_specs=[hbm] * 12,
         out_specs=(vmem, vmem),
         scratch_shapes=[
-            pltpu.VMEM((3, 2, 2 * NB + 2, ROWS + 16, 128), F32),
+            pltpu.VMEM((4, 2, 2 * NB + 2, ROWS + 16, 128), F32),
             pltpu.VMEM((2, 8, 2 * NB, 8, 128), F32),
             pltpu.VMEM((2, 8, 2 * NB, 8, 128), F32),
             pltpu.VMEM((NB, 2048, 128), F32),
-            pltpu.VMEM((NB, 512, 512), BF),
-            pltpu.VMEM((NB, 512, 512), BF),
-            pltpu.VMEM((2, 2 * ROWS, 512), BF),
+            pltpu.VMEM((NB // 2, 512, 512), BF),
+            pltpu.VMEM((NB // 2, 512, 512), BF),
+            pltpu.VMEM((NB // 2, 512, 512), BF),
+            pltpu.VMEM((NB // 2, 512, 512), BF),
+            pltpu.VMEM((2 * ROWS, 512), BF),
+            pltpu.VMEM((2 * ROWS, 512), BF),
             pltpu.VMEM((8, 2, ROWS, 128), F32),
-            pltpu.VMEM((8, 2, 8, 8, 128), F32),
+            pltpu.VMEM((8, 2, ROWS, 128), F32),
             pltpu.VMEM((2, ROWS, 128), F32),
             pltpu.VMEM((2, 2, ROWS, 128), F32),
             pltpu.VMEM((2, ROWS, 128), F32),

time: 46.2 us -> 44 us (0.952)
  Pallas kernels: 43.5 us -> 41.3 us
    pallas_call x1, Pallas kernels: 43.5 us -> 41.3 us  [per_device(): pl.pallas_call(body, out_shape=(jax.ShapeDtypeStruct((2, 8, 2 * NB, 8, 12...]
where the time goes in v2:
time: 44 us; the launch traced here: 43.9 us
  Pallas kernels  41.3 us (94%)
  local copies, waits for them, and re-layouts  1.95 us (4%)
  between operations  0.64 us (1%)
    pallas_call x1, Pallas kernels, per_device(): pl.pallas_call(body, out_shape=(jax.ShapeDtypeStruct((2, 8, 2 * NB, 8, 12...  41.3 us
    unnamed x2, local copies, waits for them, and re-layouts  1.95 us

profile of v2, /device:TPU:1, one launch (start us, length us, event | category | flops | bytes accessed | tf_op | source)
XLA Modules:
  0.0 43.9 jit_solution(3967448708530571352)
XLA Ops:
  0.6 41.3 %relax.1 = (f32[2,8,32,8,128]{4,3,2,1,0:T(8,128)S(1)}, f32[1,2,64,128]{3,2,1,0:T(8,128)S(1)}) custom-call(f32[2,8,32,8,128]{4,3,2,1,0:T(8,128)} %bitcast.23, f32[2,8,32,8,128]{4,3,2,1,0:T(8,128)} %bitcast.24, f32[1,2,64,4096]{3,2,1,0:T(8,128)} %start_hbm.1, f32[2,8,32,8,128]{4,3,2,1,0:T(8,128)} %bitcast.22, f32[16,2048,128]{2,1,0:T(8,128)} %bitcast.21, ...), custom_call_target="tpu_custom_call" | custom-call | tf_op jit(solution)/shard_map/relax/pallas_call | solution.py:505
  42.0 1.3 %copy.16 = f32[1,2,64,4096]{3,2,1,0:T(8,128)} copy(f32[1,2,64,4096]{3,2,1,0:T(8,128)S(1)} %bitcast.20) | data formatting | bytes 4194304
  43.3 0.6 %copy.17 = f32[1,2,64,128]{3,2,1,0:T(8,128)} copy(f32[1,2,64,128]{3,2,1,0:T(8,128)S(1)} %get-tuple-element.9) | data formatting | bytes 131072

commit v3 on v2

--- a/solution.py
+++ b/solution.py
@@ -12,17 +12,18 @@
 F32 = jnp.float32
 NB = 16
 ROWS = 64
-EARLY = 4
-
-EVEN = ((0, 0, 0, 2), (8, 1, 0, 2), (12, 1, 14, 0), (13, 1, 8, 2), (16, 2, 0, 2))
+EARLY = 12
+FIRST = 4
+
+EVEN = ((0, 0, 0, 2), (8, 1, 0, 2), (11, 1, 14, 0), (12, 1, 6, 2), (16, 2, 0, 2))
 ODD = (
-    (0, 0, 1, 2), (7, 1, 1, 0), (8, 0, 15, 0), (9, 1, 3, 2), (12, 1, 15, 0),
-    (13, 1, 9, 2), (16, 2, 15, 0), (17, 2, 1, 2),
+    (0, 0, 1, 2), (8, 1, 1, 2), (11, 1, 15, 0), (12, 1, 7, 2), (14, 2, 15, 0),
+    (15, 1, 11, 2), (17, 2, 1, 2),
 )
 STEPS = 24
 SPLITS = (NB - EARLY) // 2
-AT_INFLOW = 8
-AT_FAR = 16
+AT_INFLOW = 7
+AT_FAR = 14
 
 
 def static_entry(runs, m):
@@ -37,8 +38,19 @@
     assert order[2 * AT_INFLOW + 1] == (0, 15) and order[2 * AT_FAR + 1] == (2, 15)
     assert all(k % 2 == e % 2 for e, (s, k) in enumerate(order))
     assert all(order[e] == (0, e) for e in range(2 * SPLITS + 1))
+    sent = {}
+    for m in range(STEPS):
+        s, k = order[2 * m + 1]
+        if s < 2:
+            sent[(s, k // 2)] = m
+            assert max(at[(s, k - 1)], at[(s, k)]) <= 2 * m + 1
+    assert len(sent) == NB
     for s, k in order:
         if s:
+            e = at[(s, k)]
+            assert sent[(s - 1, k // 2)] < (e - 1) // 2
+            if k % 2:
+                assert (s, k) == (2, NB - 1) or at[(s, k - 1)] < e
             for j in (k - 1, k, k + 1):
                 if 0 <= j < NB:
                     assert at[(s - 1, j)] + 2 <= at[(s, k)]
@@ -120,14 +132,14 @@
     ]
     own_mult = pltpu.make_async_copy(mult_hbm.at[0], held.at[place], small_sem.at[6])
 
-    def edge_copy(side, s, k):
-        t = 2 * k + 1
+    def edge_copy(side, s, j):
+        t = 4 * j + 1
         row, there, to = ((8, line_above, above), (ROWS + 7, line_below, below))[side]
         return pltpu.make_async_remote_copy(
-            src_ref=field.at[s, :, pl.ds(t, 2), pl.ds(row, 1), :],
-            dst_ref=field.at[s, :, pl.ds(t, 2), pl.ds(there, 1), :],
+            src_ref=field.at[s, :, pl.ds(t, 4), pl.ds(row, 1), :],
+            dst_ref=field.at[s, :, pl.ds(t, 4), pl.ds(there, 1), :],
             send_sem=hs_sem.at[side, s],
-            recv_sem=hr_sem.at[side, s, k],
+            recv_sem=hr_sem.at[side, s, j],
             device_id=(sub, to),
             device_id_type=MESH,
         )
@@ -305,20 +317,27 @@
                     field[s, c, t, 8 : ROWS + 8, :] + z[:, a : a + 128]
                 )
 
-    def send_edges(s, k):
-        edge_copy(0, s, k).start()
-        edge_copy(1, s, k).start()
-
-    def await_edges(s, k):
-        edge_copy(0, s, k).wait_recv()
-        edge_copy(1, s, k).wait_recv()
+    def send_edges(s, j):
+        edge_copy(0, s, j).start()
+        edge_copy(1, s, j).start()
+
+    def await_edges(s, j):
+        edge_copy(0, s, j).wait_recv()
+        edge_copy(1, s, j).wait_recv()
 
     def column(which):
         lane = lax.broadcasted_iota(jnp.int32, (ROWS, 16), 1)
         return jnp.sum(jnp.where(lane == which, peers[...], 0.0), axis=1, keepdims=True)
 
-    await_inputs(0)
-    split(0, 0)
+    def split_pairs(start, stop):
+        @pl.loop(start // 2, stop // 2)
+        def _(i):
+            await_inputs(2 * i)
+            split(2 * i, 0)
+            await_inputs(2 * i + 1)
+            split(2 * i + 1, 1)
+
+    split_pairs(0, FIRST)
 
     pl.semaphore_wait(barrier, 10)
     first_edge(0).start()
@@ -327,9 +346,7 @@
     for offset in range(1, 8):
         spread(mult_hbm.at[0], held, s1_sem, r1_sem, offset, place).start()
 
-    for j in range(1, EARLY):
-        await_inputs(j)
-        split(j, j % 2)
+    split_pairs(FIRST, EARLY)
 
     @pl.loop(0, EARLY)
     def _(j):
@@ -364,13 +381,12 @@
         z = product(e + 1, 1)
         split(e + EARLY, 0)
         update(0, e + 1, z)
-        send_edges(1, e)
-        send_edges(1, e + 1)
+        send_edges(1, m)
 
     def later(m, carry):
         s0, k0, s1, k1, s2, k2 = carry
 
-        @pl.when(m == AT_INFLOW - 1)
+        @pl.when(m == AT_INFLOW - 2)
         def _():
             for offset in range(1, 8):
                 j = lax.rem(place + offset, places)
@@ -397,13 +413,13 @@
                 total = inflow[c] + part_in[c]
                 src[c, :, 2 * NB - 1] = src[c, :, 2 * NB - 1] + total.reshape(8, 8, 128)
 
-        @pl.when(s1 > 0)
+        @pl.when(m == AT_FAR)
         def _():
-            await_edges(s1, k1)
-
-        @pl.when(s2 > 0)
+            await_edges(2, NB // 2 - 1)
+
+        @pl.when((s2 > 0) & ((s2 < 2) | (k2 < NB - 2)))
         def _():
-            await_edges(s2, k2)
+            await_edges(s2, k2 // 2)
 
         s3, k3 = entry_of(ODD, m + 1)
         s4, k4 = entry_of(EVEN, m + 2)
@@ -412,13 +428,9 @@
         residual(s2, k2, lhs_even)
         update(s1, k1, product(k1, 1))
 
-        @pl.when(s0 < 2)
-        def _():
-            send_edges(s0 + 1, k0)
-
         @pl.when(s1 < 2)
         def _():
-            send_edges(s1 + 1, k1)
+            send_edges(s1 + 1, k1 // 2)
 
         @pl.when(m == AT_FAR)
         def _():
@@ -433,7 +445,6 @@
         (*entry_of(EVEN, first), *entry_of(ODD, first), *entry_of(EVEN, first + 1)),
     )
     s, k = static_entry(ODD, STEPS - 1)
-    await_edges(s, k)
     residual(s, k, lhs_odd)
     s0, k0 = static_entry(EVEN, STEPS - 1)
     update(s0, k0, product(k0, 0))
@@ -539,7 +550,7 @@
             dma((NB,)),
             dma((7,)),
             dma((2, 3)),
-            dma((2, 3, NB)),
+            dma((2, 3, NB // 2)),
             dma((7,)),
             dma((8,)),
             dma((7,)),

time: 44 us -> 42.4 us (0.964)
  Pallas kernels: 41.3 us -> 39.7 us
    pallas_call x1, Pallas kernels: 41.3 us -> 39.7 us  [per_device(): pl.pallas_call(body, out_shape=(jax.ShapeDtypeStruct((2, 8, 2 * NB, 8, 12...]
where the time goes in v3:
time: 42.4 us; the launch traced here: 42.3 us
  Pallas kernels  39.7 us (94%)
  local copies, waits for them, and re-layouts  1.95 us (5%)
  between operations  0.64 us (2%)
    pallas_call x1, Pallas kernels, per_device(): pl.pallas_call(body, out_shape=(jax.ShapeDtypeStruct((2, 8, 2 * NB, 8, 12...  39.7 us
    unnamed x2, local copies, waits for them, and re-layouts  1.95 us

profile of v3, /device:TPU:1, one launch (start us, length us, event | category | flops | bytes accessed | tf_op | source)
XLA Modules:
  0.0 42.3 jit_solution(18062571287729511236)
XLA Ops:
  0.6 39.7 %relax.1 = (f32[2,8,32,8,128]{4,3,2,1,0:T(8,128)S(1)}, f32[1,2,64,128]{3,2,1,0:T(8,128)S(1)}) custom-call(f32[2,8,32,8,128]{4,3,2,1,0:T(8,128)} %bitcast.23, f32[2,8,32,8,128]{4,3,2,1,0:T(8,128)} %bitcast.24, f32[1,2,64,4096]{3,2,1,0:T(8,128)} %start_hbm.1, f32[2,8,32,8,128]{4,3,2,1,0:T(8,128)} %bitcast.22, f32[16,2048,128]{2,1,0:T(8,128)} %bitcast.21, ...), custom_call_target="tpu_custom_call" | custom-call | tf_op jit(solution)/shard_map/relax/pallas_call | solution.py:516
  40.3 1.3 %copy.16 = f32[1,2,64,4096]{3,2,1,0:T(8,128)} copy(f32[1,2,64,4096]{3,2,1,0:T(8,128)S(1)} %bitcast.20) | data formatting | bytes 4194304
  41.6 0.6 %copy.17 = f32[1,2,64,128]{3,2,1,0:T(8,128)} copy(f32[1,2,64,128]{3,2,1,0:T(8,128)S(1)} %get-tuple-element.9) | data formatting | bytes 131072

commit v4 on v3

--- a/solution.py
+++ b/solution.py
@@ -13,17 +13,20 @@
 NB = 16
 ROWS = 64
 EARLY = 12
-FIRST = 4
-
-EVEN = ((0, 0, 0, 2), (8, 1, 0, 2), (11, 1, 14, 0), (12, 1, 6, 2), (16, 2, 0, 2))
+FIRST = 2
+
+EVEN = (
+    (0, 0, 0, 2), (4, 0, 14, 0), (5, 0, 8, 2), (8, 1, 0, 0), (9, 1, 14, 0), (10, 1, 2, 2),
+    (16, 2, 0, 2),
+)
 ODD = (
-    (0, 0, 1, 2), (8, 1, 1, 2), (11, 1, 15, 0), (12, 1, 7, 2), (14, 2, 15, 0),
-    (15, 1, 11, 2), (17, 2, 1, 2),
+    (0, 0, 1, 2), (4, 0, 15, 0), (5, 0, 9, 2), (8, 1, 1, 0), (9, 1, 15, 0), (10, 1, 3, 2),
+    (13, 2, 15, 0), (14, 1, 9, 2), (17, 2, 1, 2),
 )
 STEPS = 24
 SPLITS = (NB - EARLY) // 2
-AT_INFLOW = 7
-AT_FAR = 14
+AT_INFLOW = 4
+AT_FAR = 13
 
 
 def static_entry(runs, m):
@@ -179,20 +182,20 @@
     def far_source():
         return field.at[3, :, 2 * NB, pl.ds(8, ROWS), :]
 
+    barrier = pltpu.get_barrier_semaphore()
+    for offset in range(1, 8):
+        to = lax.rem(place + offset, places)
+        pl.semaphore_signal(barrier, inc=1, device_id=(to * 2 + core, tile), device_id_type=MESH)
+    pl.semaphore_signal(barrier, inc=1, device_id=(partner, tile), device_id_type=MESH)
+
+    pl.semaphore_signal(barrier, inc=1, device_id=(sub, above), device_id_type=MESH)
+    pl.semaphore_signal(barrier, inc=1, device_id=(sub, below), device_id_type=MESH)
+
     for copy in small:
         copy.start()
     for j in range(2):
         issue(j)
     own_mult.start()
-    barrier = pltpu.get_barrier_semaphore()
-    for offset in range(1, 8):
-        to = lax.rem(place + offset, places)
-        pl.semaphore_signal(barrier, inc=1, device_id=(to * 2 + core, tile), device_id_type=MESH)
-    pl.semaphore_signal(barrier, inc=1, device_id=(partner, tile), device_id_type=MESH)
-
-    pl.semaphore_signal(barrier, inc=1, device_id=(sub, above), device_id_type=MESH)
-    pl.semaphore_signal(barrier, inc=1, device_id=(sub, below), device_id_type=MESH)
-
     @pl.loop(2, NB)
     def _(j):
         issue(j)
@@ -456,19 +459,20 @@
     own_peer = column(sub)
     their_peer = column(partner)
     far[place] = field[3, :, 2 * NB, 8 : ROWS + 8, :]
-    for offset in range(1, 8):
+    mine = [jnp.zeros((ROWS, 128), F32)] * 2
+    theirs = [jnp.zeros((ROWS, 128), F32)] * 2
+    for offset in range(8, 0, -1):
         j = lax.rem(place + offset, places)
-        spread(far_source(), far, s2_sem, r2_sem, offset, j).wait_recv()
+        if offset < 8:
+            spread(far_source(), far, s2_sem, r2_sem, offset, j).wait_recv()
+        at = (2 * j + core).astype(F32)
+        for c in range(2):
+            v = far[j, c]
+            mine[c] = mine[c] + jnp.where(own_peer == at, v, 0.0)
+            theirs[c] = theirs[c] + jnp.where(their_peer == at, v, 0.0)
     for c in range(2):
-        mine = jnp.zeros((ROWS, 128), F32)
-        theirs = jnp.zeros((ROWS, 128), F32)
-        for j in range(8):
-            v = far[j, c]
-            at = (2 * j + core).astype(F32)
-            mine = mine + jnp.where(own_peer == at, v, 0.0)
-            theirs = theirs + jnp.where(their_peer == at, v, 0.0)
-        inflow[c] = mine
-        part[1, c] = theirs
+        inflow[c] = mine[c]
+        part[1, c] = theirs[c]
     to_partner(part.at[1], end_in, 1).start()
     to_partner(part.at[1], end_in, 1).wait_recv()
     for c in range(2):

time: 42.4 us -> 42.2 us (level)
  no operation moved by 1% of the time
where the time goes in v4:
time: 42.2 us; the launch traced here: 42.1 us
  Pallas kernels  39.5 us (94%)
  local copies, waits for them, and re-layouts  1.95 us (5%)
  between operations  0.64 us (2%)
    pallas_call x1, Pallas kernels, per_device(): pl.pallas_call(body, out_shape=(jax.ShapeDtypeStruct((2, 8, 2 * NB, 8, 12...  39.5 us
    unnamed x2, local copies, waits for them, and re-layouts  1.95 us

profile of v4, /device:TPU:1, one launch (start us, length us, event | category | flops | bytes accessed | tf_op | source)
XLA Modules:
  0.0 42.1 jit_solution(10993174048244497690)
XLA Ops:
  0.6 39.5 %relax.1 = (f32[2,8,32,8,128]{4,3,2,1,0:T(8,128)S(1)}, f32[1,2,64,128]{3,2,1,0:T(8,128)S(1)}) custom-call(f32[2,8,32,8,128]{4,3,2,1,0:T(8,128)} %bitcast.23, f32[2,8,32,8,128]{4,3,2,1,0:T(8,128)} %bitcast.24, f32[1,2,64,4096]{3,2,1,0:T(8,128)} %start_hbm.1, f32[2,8,32,8,128]{4,3,2,1,0:T(8,128)} %bitcast.22, f32[16,2048,128]{2,1,0:T(8,128)} %bitcast.21, ...), custom_call_target="tpu_custom_call" | custom-call | tf_op jit(solution)/shard_map/relax/pallas_call | solution.py:520
  40.1 1.3 %copy.16 = f32[1,2,64,4096]{3,2,1,0:T(8,128)} copy(f32[1,2,64,4096]{3,2,1,0:T(8,128)S(1)} %bitcast.20) | data formatting | bytes 4194304
  41.4 0.6 %copy.17 = f32[1,2,64,128]{3,2,1,0:T(8,128)} copy(f32[1,2,64,128]{3,2,1,0:T(8,128)S(1)} %get-tuple-element.9) | data formatting | bytes 131072
